TPU v7x, 256 devices: a whole 4x4x8 slice. The times are simulated.
256 devices in a mesh: cell: 8 (over z_hi, x), seq: 32 (over z_lo, y, core).
Axes of the slice: x: 4, y: 4, z: 8 (z_hi: 2, z_lo: 4; z = z_hi * 4 + z_lo), core: 2. Of those that a mesh axis runs over, the one named last changes fastest.
Arguments:
- features: bfloat16 [8192, 1536], P('seq', 'cell'), may hold values from -6 to 6
- w_qkv: bfloat16 [1536, 768], replicated, may hold values from -0.15625 to 0.15625
- buckets: int32 [8, 64, 16], P('cell', 'seq'), may hold values from 0 to 31
- cell_ids: int32 [8], P('cell'), may hold values from 0 to 31
- bias_table: float32 [32, 32, 2], replicated, may hold values from -8 to 330
- d_attended: bfloat16 [8, 8192, 256], P('cell', 'seq'), may hold values from -6 to 6
Outputs:
- attended: bfloat16 [8, 8192, 256], P('cell', 'seq')
- grad_qkv: float32 [1536, 768], P('cell')
- grad_table: float32 [32, 32, 2], replicated
All inputs are finite; a program needn't handle non-finite values.
Results may differ from a plain program's by a relative error of at most 0.02.
Values may be sent and summed in bfloat16 or wider, within the bound.
A program may use at most 64 MiB of HBM per device.

v0:
```python
import math
import jax
import jax.numpy as jnp
from jax import lax
from jax.sharding import PartitionSpec as P

HEADS = 2
HD = 128
TILE = 128
BT = 16


def passed_along(block, axis, distance):
    devices = range(lax.axis_size(axis))
    route = [(i - distance, i) for i in devices if i - distance in devices]
    return lax.ppermute(block, axis, route)


def tile_bias(bucket_rows, table_row, query_tiles, key_first, key_count, tile_total):
    band_width = bucket_rows.shape[1]
    middle = band_width // 2
    key_tiles = (key_first + jnp.arange(key_count, dtype=jnp.int32)) // TILE
    offsets = key_tiles[None, :] - query_tiles[:, None] + middle
    key_valid = (key_tiles >= 0) & (key_tiles < tile_total)
    query_valid = (query_tiles >= 0) & (query_tiles < tile_total)
    inside = (offsets >= 0) & (offsets < band_width) & key_valid[None, :] & query_valid[:, None]
    matches = offsets[:, :, None] == jnp.arange(band_width, dtype=jnp.int32)[None, None, :]
    bucket_ids = jnp.sum(jnp.where(matches, bucket_rows[:, None, :], 0), axis=2)
    levels = table_row.shape[0]
    onehot = (bucket_ids[:, :, None] == jnp.arange(levels, dtype=jnp.int32)[None, None, :]).astype(
        jnp.float32
    )
    bias_terms = jnp.einsum("qkb,bh->qhk", onehot, table_row, precision=lax.Precision.HIGHEST)
    return (bias_terms, inside, onehot)


def band_scores(query_rows, key_rows, bias_terms, inside, factor):
    raw_scores = jnp.einsum(
        "qhd,khd->qhk", query_rows, key_rows, preferred_element_type=jnp.float32
    )
    tile_count = bias_terms.shape[0]
    shaped = raw_scores.reshape(tile_count, TILE, raw_scores.shape[1], raw_scores.shape[2]) * factor
    shaped = shaped + bias_terms[:, None]
    keep_mask = jnp.broadcast_to(inside[:, None, None, :], shaped.shape)
    shaped = jnp.where(keep_mask, shaped, -1e30)
    return (shaped.reshape(raw_scores.shape), keep_mask.reshape(raw_scores.shape))


def fetch_keys(block, offset):
    return passed_along(block, "seq", -offset)


def return_grads(block, offset):
    return passed_along(block, "seq", offset)


def local(features, w_qkv, buckets, cell_ids, bias_table, d_attended):
    row_count = features.shape[0]
    width_part = features.shape[1]
    inner_width = HEADS * HD
    seq_count = lax.axis_size("seq")
    total_rows = row_count * seq_count
    tile_total = total_rows // TILE
    factor = 1.0 / math.sqrt(HD)
    seq_pos = lax.axis_index("seq")
    tiles_here = row_count // TILE
    half_band = BT * TILE // 2
    reach = min((half_band + row_count - 1) // row_count, seq_count - 1)
    span = 2 * reach + 1
    window_first = (seq_pos - reach) * row_count
    query_tiles = seq_pos * tiles_here + jnp.arange(tiles_here, dtype=jnp.int32)
    cell_pos = lax.axis_index("cell")
    weight_rows = lax.dynamic_slice_in_dim(w_qkv, cell_pos * width_part, width_part, 0)
    partial_qkv = jnp.dot(features, weight_rows, preferred_element_type=jnp.float32)
    projected = lax.psum(partial_qkv, "cell").astype(jnp.bfloat16)
    queries_flat = projected[:, :inner_width]
    queries = queries_flat.reshape(row_count, HEADS, HD)
    queries_wide = queries.astype(jnp.float32)
    key_value = projected[:, inner_width:]
    window_pieces = []
    for offset in range(-reach, reach + 1):
        if offset == 0:
            window_pieces.append(key_value)
        else:
            window_pieces.append(fetch_keys(key_value, offset))
    window_kv = jnp.concatenate(window_pieces, axis=0)
    window_keys = window_kv[:, :inner_width].reshape(span * row_count, HEADS, HD)
    window_values = window_kv[:, inner_width:].reshape(span * row_count, HEADS, HD)
    type_hit = jnp.arange(bias_table.shape[0], dtype=jnp.int32) == cell_ids[0]
    table_row = jnp.sum(jnp.where(type_hit[:, None, None], bias_table, 0.0), axis=0)
    bucket_rows = buckets[0]

    def block_terms(block_index):
        local_first = block_index * row_count
        key_blk = lax.dynamic_slice_in_dim(window_keys, local_first, row_count, 0)
        value_blk = lax.dynamic_slice_in_dim(window_values, local_first, row_count, 0)
        bias_terms, inside, onehot = tile_bias(
            bucket_rows, table_row, query_tiles, window_first + local_first, row_count, tile_total
        )
        scores, keep_mask = band_scores(queries, key_blk, bias_terms, inside, factor)
        return (key_blk, value_blk, scores, keep_mask, onehot)

    def stats_step(block_index, loop_carry):
        row_top, row_mass = loop_carry
        scores, keep_mask = block_terms(block_index)[2:4]
        new_top = jnp.maximum(row_top, jnp.max(scores, axis=2))
        fresh = jnp.sum(jnp.where(keep_mask, jnp.exp(scores - new_top[:, :, None]), 0.0), axis=2)
        return (new_top, row_mass * jnp.exp(row_top - new_top) + fresh)

    start_top = jnp.full((row_count, HEADS), -1e30, jnp.float32)
    start_mass = jnp.zeros((row_count, HEADS), jnp.float32)
    row_top, row_mass = lax.fori_loop(0, span, stats_step, (start_top, start_mass))
    log_total = row_top + jnp.log(row_mass)

    def value_step(block_index, value_sum):
        value_blk, scores, keep_mask = block_terms(block_index)[1:4]
        weights = jnp.where(keep_mask, jnp.exp(scores - log_total[:, :, None]), 0.0).astype(
            jnp.bfloat16
        )
        return value_sum + jnp.einsum(
            "qhk,khd->qhd", weights, value_blk, preferred_element_type=jnp.float32
        )

    value_sum = lax.fori_loop(0, span, value_step, jnp.zeros((row_count, HEADS, HD), jnp.float32))
    attended = value_sum.astype(jnp.bfloat16)
    grad_flat = d_attended[0]
    grad_out = grad_flat.reshape(row_count, HEADS, HD)
    row_delta = jnp.sum(grad_out.astype(jnp.float32) * attended.astype(jnp.float32), axis=2)
    levels = bias_table.shape[1]

    def grad_core(block_index):
        key_blk, value_blk, scores, keep_mask, onehot = block_terms(block_index)
        chance = jnp.where(keep_mask, jnp.exp(scores - log_total[:, :, None]), 0.0)
        chance_b = chance.astype(jnp.bfloat16)
        grad_push = jnp.einsum(
            "qhd,khd->qhk", grad_out, value_blk, preferred_element_type=jnp.float32
        )
        dscore = chance * (grad_push - row_delta[:, :, None])
        q_part = jnp.einsum(
            "qhk,khd->qhd",
            dscore,
            key_blk.astype(jnp.float32),
            precision=lax.Precision.HIGHEST,
            preferred_element_type=jnp.float32,
        )
        tile_sum = dscore.reshape(tiles_here, TILE, HEADS, row_count).sum(axis=1)
        table_part = jnp.einsum("qhk,qkb->bh", tile_sum, onehot, precision=lax.Precision.HIGHEST)
        return (chance_b, dscore, q_part, table_part)

    zero_rows = jnp.zeros((row_count, HEADS, HD), jnp.float32)
    zero_table = jnp.zeros((levels, HEADS), jnp.float32)

    def grad_step(block_index, loop_carry):
        q_total, table_total, key_store = loop_carry
        chance_b, dscore, q_part, table_part = grad_core(block_index)
        key_part = (
            jnp.einsum(
                "qhk,qhd->khd",
                dscore,
                queries_wide,
                precision=lax.Precision.HIGHEST,
                preferred_element_type=jnp.float32,
            )
            * factor
        )
        value_part = jnp.einsum(
            "qhk,qhd->khd", chance_b, grad_out, preferred_element_type=jnp.float32
        )
        merged = jnp.concatenate(
            [key_part.reshape(row_count, inner_width), value_part.reshape(row_count, inner_width)],
            axis=1,
        )
        key_store = lax.dynamic_update_slice_in_dim(key_store, merged, block_index * row_count, 0)
        return (q_total + q_part, table_total + table_part, key_store)

    key_store = jnp.zeros((span * row_count, 2 * inner_width), jnp.float32)
    q_total, table_total, key_store = lax.fori_loop(
        0, span, grad_step, (zero_rows, zero_table, key_store)
    )
    key_grads = key_store[reach * row_count : (reach + 1) * row_count]
    for slot_index in range(span):
        offset = slot_index - reach
        if offset != 0:
            segment = key_store[slot_index * row_count : (slot_index + 1) * row_count]
            key_grads = key_grads + return_grads(segment, offset)
    query_grads = (q_total * factor).reshape(row_count, inner_width)
    row_grads = jnp.concatenate([query_grads, key_grads], axis=1)
    summed_rows = lax.psum(row_grads, "cell")
    share = jnp.dot(
        features.astype(jnp.float32).T,
        summed_rows,
        precision=lax.Precision.HIGHEST,
        preferred_element_type=jnp.float32,
    )
    grad_qkv = lax.psum(share, "seq")
    table_term = jnp.where(type_hit[:, None, None], table_total[None, :, :], 0.0)
    grad_table = lax.psum(table_term, ("cell", "seq"))
    return (attended.reshape(1, row_count, inner_width), grad_qkv, grad_table)


def solution(mesh):
    in_specs = (
        P("seq", "cell"),
        P(),
        P("cell", "seq", None),
        P("cell"),
        P(),
        P("cell", "seq", None),
    )
    out_specs = (P("cell", "seq", None), P("cell", None), P())
    return jax.shard_map(local, mesh=mesh, in_specs=in_specs, out_specs=out_specs, check_vma=False)
```

profile of v0, /device:TPU:2, one launch (start us, length us, event | category | flops | bytes accessed | tf_op | source)
XLA Modules:
  0.0 758.4 jit_solution(12148896757726910611)
XLA Ops:
  7.3 1.6 copy-done
  10.0 63.3 %all-reduce.7 = bf16[256,768]{0,1:T(8,128)(2,1)} all-reduce(f32[256,768]{0,1:T(8,128)S(1)} %convolution_bitcast_fusion.6), channel_id=1, replica_groups=mesh['cell'=8,'seq'=32] {'cell'}, use_global_device_ids=true, to_apply=%region_0.0 | all-reduce | flops 196608 | bytes 1179648 | tf_op jit(solution)/shard_map/psum | solution.py:75
  74.4 5.8 collective-permute-start
  82.8 3.3 collective-permute-start.2
  86.1 4.0 collective-permute-start.1
  93.9 5.3 collective-permute-start.3
  100.3 2.1 collective-permute-done.1
  108.1 5.0 collective-permute-done.5
  114.2 1.6 fusion.66
  115.7 2.4 copy.86
  118.1 48.4 %while.54 = (s32[]{:T(128)}, f32[256,2]{0,1:T(2,128)S(1)}, f32[256,2]{0,1:T(2,128)S(1)}, s32[]{:T(128)}, bf16[2304,2,128]{2,0,1:T(8,128)(2,1)}, /*index=5*/bf16[...) while((s32[]{:T(128)}, f32[256,2]{0,1:T(2,128)S(1)}, ...), condition=%wide.region_6.7_spmd.clone, body=%wide.region_2.6_spmd.clone.sunk | while | flops 34921744 | bytes 3791994 | solution.py:112
  166.5 51.4 %while.55 = (s32[]{:T(128)}, f32[256,2,128]{0,2,1:T(8,128)}, bf16[2304,2,128]{0,2,1:T(8,128)(2,1)}, s32[]{:T(128)}, bf16[2304,2,128]{2,0,1:T(8,128)(2,1)}, /*ind...) while((s32[]{:T(128)}, f32[256,2,128]{0,2,1:T(8,128)}, ...), condition=%wide.region_9.10_spmd.clone, body=%wide.region_7.9_spmd.clone.sunk | while | flops 68473616 | bytes 3834520 | solution.py:124
  169.9 2.4 fusion.112
  175.5 2.4 fusion.112
  181.2 2.4 fusion.112
  186.9 2.4 fusion.112
  192.7 2.4 fusion.112
  198.4 2.4 fusion.112
  204.1 2.4 fusion.112
  209.8 2.4 fusion.112
  215.5 2.4 fusion.112
  219.0 2.4 broadcast_in_dim.354
  221.4 60.5 %while.56 = (s32[]{:T(128)}, f32[256,2,128]{0,2,1:T(8,128)S(1)}, f32[32,2]{0,1:T(2,128)S(1)}, f32[2304,512]{0,1:T(8,128)}, bf16[2304,2,128]{2,0,1:T(8,128)(2,1)}...) while((s32[]{:T(128)}, f32[256,2,128]{0,2,1:T(8,128)S(1)}, ...), condition=%wide.region_14.15_spmd.clone, body=%wide.region_11.14_spmd.clone.sunk | while | flops 505679744 | bytes 7515830 | solution.py:177
  225.4 1.4 fusion.125
  232.1 1.4 fusion.125
  238.9 1.4 fusion.125
  245.6 1.4 fusion.125
  252.3 1.4 fusion.125
  259.1 1.4 fusion.125
  265.8 1.4 fusion.125
  272.5 1.4 fusion.125
  279.2 1.4 fusion.125
  281.9 2.6 fusion.65
  284.6 1.3 collective-permute-start.8
  285.9 4.4 collective-permute-start.13
  290.3 4.3 collective-permute-start.12
  297.2 5.6 collective-permute-done.8
  304.1 8.0 %collective-permute-done.13 = f32[256,512]{0,1:T(8,128)S(1)} collective-permute-done((f32[256,512]{0,1:T(8,128)S(1)}, f32[256,512]{0,1:T(8,128)S(1)}, u32[]{:S(2)}, u32[]{:S(2)}) %collective-permute-start.13) | collective-permute-done | bytes 524320 | tf_op jit(solution)/shard_map/ppermute | solution.py:16
  312.1 8.6 %collective-permute-start.15 = (f32[256,512]{0,1:T(8,128)S(1)}, f32[256,512]{0,1:T(8,128)S(1)}, u32[]{:S(2)}, u32[]{:S(2)}) collective-permute-start(f32[256,512]{0,1:T(8,128)S(1)} %get-tuple-element.1199), channel_id=1, source_target_pairs={{0,4},{1,5},{2,6},{3,7},{4,8},{5,9},{6,10},{7,11},{8,12},{9,13},{1... | collective-permute-start | bytes 1572872 | tf_op jit(solution)/shard_map/ppermute | solution.py:16
  320.7 3.4 collective-permute-start.14
  324.1 10.8 %collective-permute-done.10 = f32[256,512]{0,1:T(8,128)S(1)} collective-permute-done((f32[256,512]{0,1:T(8,128)S(1)}, f32[256,512]{0,1:T(8,128)S(1)}, u32[]{:S(2)}, u32[]{:S(2)}) %collective-permute-start.10) | collective-permute-done | bytes 524320 | tf_op jit(solution)/shard_map/ppermute | solution.py:16
  335.1 14.4 %collective-permute-done.14 = f32[256,512]{0,1:T(8,128)S(1)} collective-permute-done((f32[256,512]{0,1:T(8,128)S(1)}, f32[256,512]{0,1:T(8,128)S(1)}, u32[]{:S(2)}, u32[]{:S(2)}) %collective-permute-start.14) | collective-permute-done | bytes 524320 | tf_op jit(solution)/shard_map/ppermute | solution.py:16
  349.6 1.4 add_add_fusion
  352.0 123.4 %all-reduce.4.cloned.1.call-done = f32[256,768]{0,1:T(8,128)} async-done(((f32[256,768]{0,1:T(8,128)}), f32[256,768]{0,1:T(8,128)}) %all-reduce.4.cloned.1.call-update) | async-done | bytes 786448 | tf_op jit(solution)/shard_map/psum | solution.py:188
  475.4 2.5 convolution_bitcast_fusion.7
  478.9 77.6 %psum.31 = f32[32,32,2]{1,2,0:T(2,128)} all-reduce(f32[32,32,2]{1,2,0:T(2,128)S(1)} %broadcast_select_fusion.1), channel_id=1, replica_groups=mesh['cell'=8,'seq'=32] {'cell','seq'}, use_global_device_ids=true, to_apply=%region_17.18 | all-reduce | flops 2048 | bytes 16384 | tf_op jit(solution)/shard_map/psum | solution.py:197
  556.4 193.2 %all-reduce.6.cloned.1.call-done = f32[192,768]{1,0:T(8,128)} async-done(((f32[192,768]{1,0:T(8,128)}), f32[192,768]{1,0:T(8,128)}) %all-reduce.6.cloned.1.call-update) | async-done | bytes 589840 | tf_op jit(solution)/shard_map/psum | solution.py:195
  749.6 1.9 copy.153
  (518 shorter events, 146.8 us)
Async XLA Ops:
  7.2 1.7 copy-start
  7.2 83.6 %copy-start.9 = (f32[32,32,2]{1,2,0:T(2,128)S(1)}, f32[32,32,2]{1,2,0:T(2,128)}, u32[]{:S(2)}) copy-start(f32[32,32,2]{1,2,0:T(2,128)} %param.16) | copy-start | bytes 24580
  7.2 86.6 %copy-start.8 = (bf16[1,256,256]{2,1,0:T(8,128)(2,1)S(1)}, bf16[1,256,256]{2,1,0:T(8,128)(2,1)}, u32[]{:S(2)}) copy-start(bf16[1,256,256]{2,1,0:T(8,128)(2,1)} %param.17) | copy-start | bytes 393220
  7.2 468.2 %all-reduce.4.cloned.1.call-start = ((), (), s32[]{:S(2)}) async-start(), calls=%async_computation | async-start | bytes 1572864 | tf_op jit(solution)/shard_map/psum | solution.py:188
  73.3 33.6 %copy-start.5 = (bf16[256,768]{0,1:T(8,128)(2,1)S(1)}, bf16[256,768]{0,1:T(8,128)(2,1)}, u32[]{:S(2)}) copy-start(bf16[256,768]{0,1:T(8,128)(2,1)} %all-reduce.7) | copy-start | bytes 1179652
  74.4 19.6 %collective-permute-start = (bf16[256,512]{0,1:T(8,128)(2,1)S(1)}, bf16[256,512]{0,1:T(8,128)(2,1)}, u32[]{:S(2)}, u32[]{:S(2)}) collective-permute-start(bf16[256,512]{0,1:T(8,128)(2,1)S(1)} %slice.52), channel_id=1, source_target_pairs={{0,4},{1,5},{2,6},{3,7},{4,8},{5,9},{6,10},{7,11},{8,12},{9,13},{1... | collective-permute-start | bytes 786440 | tf_op jit(solution)/shard_map/ppermute | solution.py:16
  80.2 33.9 %collective-permute-start.7 = (bf16[256,512]{0,1:T(8,128)(2,1)S(1)}, bf16[256,512]{0,1:T(8,128)(2,1)S(1)}, u32[]{:S(2)}, u32[]{:S(2)}) collective-permute-start(bf16[256,512]{0,1:T(8,128)(2,1)S(1)} %slice.52), channel_id=1, source_target_pairs={{4,0},{5,1},{6,2},{7,3},{8,4},{9,5},{10,6},{11,7},{12,8},{13,9},{1... | collective-permute-start | bytes 786440 | tf_op jit(solution)/shard_map/ppermute | solution.py:16
  81.5 31.7 %collective-permute-start.6 = (bf16[256,512]{0,1:T(8,128)(2,1)S(1)}, bf16[256,512]{0,1:T(8,128)(2,1)}, u32[]{:S(2)}, u32[]{:S(2)}) collective-permute-start(bf16[256,512]{0,1:T(8,128)(2,1)S(1)} %slice.52), channel_id=1, source_target_pairs={{3,0},{4,1},{5,2},{6,3},{7,4},{8,5},{9,6},{10,7},{11,8},{12,9},{13... | collective-permute-start | bytes 786440 | tf_op jit(solution)/shard_map/ppermute | solution.py:16
  82.8 21.8 %collective-permute-start.2 = (bf16[256,512]{0,1:T(8,128)(2,1)S(1)}, bf16[256,512]{0,1:T(8,128)(2,1)}, u32[]{:S(2)}, u32[]{:S(2)}) collective-permute-start(bf16[256,512]{0,1:T(8,128)(2,1)S(1)} %slice.52), channel_id=1, source_target_pairs={{0,2},{1,3},{2,4},{3,5},{4,6},{5,7},{6,8},{7,9},{8,10},{9,11},{10,... | collective-permute-start | bytes 786440 | tf_op jit(solution)/shard_map/ppermute | solution.py:16
  86.1 16.3 %collective-permute-start.1 = (bf16[256,512]{0,1:T(8,128)(2,1)S(1)}, bf16[256,512]{0,1:T(8,128)(2,1)}, u32[]{:S(2)}, u32[]{:S(2)}) collective-permute-start(bf16[256,512]{0,1:T(8,128)(2,1)S(1)} %slice.52), channel_id=1, source_target_pairs={{0,3},{1,4},{2,5},{3,6},{4,7},{5,8},{6,9},{7,10},{8,11},{9,12},{10... | collective-permute-start | bytes 786440 | tf_op jit(solution)/shard_map/ppermute | solution.py:16
  93.9 12.9 %collective-permute-start.3 = (bf16[256,512]{0,1:T(8,128)(2,1)S(1)}, bf16[256,512]{0,1:T(8,128)(2,1)S(1)}, u32[]{:S(2)}, u32[]{:S(2)}) collective-permute-start(bf16[256,512]{0,1:T(8,128)(2,1)S(1)} %slice.52), channel_id=1, source_target_pairs={{0,1},{1,2},{2,3},{3,4},{4,5},{5,6},{6,7},{7,8},{8,9},{9,10},{10,1... | collective-permute-start | bytes 786440 | tf_op jit(solution)/shard_map/ppermute | solution.py:16
  102.3 10.8 %collective-permute-start.5 = (bf16[256,512]{0,1:T(8,128)(2,1)S(1)}, bf16[256,512]{0,1:T(8,128)(2,1)S(1)}, u32[]{:S(2)}, u32[]{:S(2)}) collective-permute-start(bf16[256,512]{0,1:T(8,128)(2,1)S(1)} %slice.52), channel_id=1, source_target_pairs={{2,0},{3,1},{4,2},{5,3},{6,4},{7,5},{8,6},{9,7},{10,8},{11,9},{12,... | collective-permute-start | bytes 786440 | tf_op jit(solution)/shard_map/ppermute | solution.py:16
  104.6 3.4 collective-permute-start.4
  115.7 2.4 copy-start.7
  166.5 3.3 copy-start.1
  172.2 3.3 copy-start.1
  177.9 3.3 copy-start.1
  183.6 3.3 copy-start.1
  189.4 3.3 copy-start.1
  195.1 3.3 copy-start.1
  200.8 3.3 copy-start.1
  206.5 3.3 copy-start.1
  212.2 3.3 copy-start.1
  218.9 2.5 copy-start.2
  218.9 2.5 copy-start.3
  219.0 2.5 copy-start.4
  219.0 2.5 copy-start.10
  284.6 18.3 %collective-permute-start.8 = (f32[256,512]{0,1:T(8,128)S(1)}, f32[256,512]{0,1:T(8,128)S(1)}, u32[]{:S(2)}, u32[]{:S(2)}) collective-permute-start(f32[256,512]{0,1:T(8,128)S(1)} %get-tuple-element.1193), channel_id=1, source_target_pairs={{4,0},{5,1},{6,2},{7,3},{8,4},{9,5},{10,6},{11,7},{12,8},{13,9},{1... | collective-permute-start | bytes 1572872 | tf_op jit(solution)/shard_map/ppermute | solution.py:16
  285.9 26.2 %collective-permute-start.13 = (f32[256,512]{0,1:T(8,128)S(1)}, f32[256,512]{0,1:T(8,128)S(1)}, u32[]{:S(2)}, u32[]{:S(2)}) collective-permute-start(f32[256,512]{0,1:T(8,128)S(1)} %get-tuple-element.1194), channel_id=1, source_target_pairs={{0,2},{1,3},{2,4},{3,5},{4,6},{5,7},{6,8},{7,9},{8,10},{9,11},{10,... | collective-permute-start | bytes 1572872 | tf_op jit(solution)/shard_map/ppermute | solution.py:16
  290.3 30.4 %collective-permute-start.12 = (f32[256,512]{0,1:T(8,128)S(1)}, f32[256,512]{0,1:T(8,128)S(1)}, u32[]{:S(2)}, u32[]{:S(2)}) collective-permute-start(f32[256,512]{0,1:T(8,128)S(1)} %get-tuple-element.1195), channel_id=1, source_target_pairs={{0,1},{1,2},{2,3},{3,4},{4,5},{5,6},{6,7},{7,8},{8,9},{9,10},{10,1... | collective-permute-start | bytes 1572872 | tf_op jit(solution)/shard_map/ppermute | solution.py:16
  294.6 29.5 %collective-permute-start.11 = (f32[256,512]{0,1:T(8,128)S(1)}, f32[256,512]{0,1:T(8,128)S(1)}, u32[]{:S(2)}, u32[]{:S(2)}) collective-permute-start(f32[256,512]{0,1:T(8,128)S(1)} %get-tuple-element.1196), channel_id=1, source_target_pairs={{1,0},{2,1},{3,2},{4,3},{5,4},{6,5},{7,6},{8,7},{9,8},{10,9},{11,1... | collective-permute-start | bytes 1572872 | tf_op jit(solution)/shard_map/ppermute | solution.py:16
  295.9 39.0 %collective-permute-start.10 = (f32[256,512]{0,1:T(8,128)S(1)}, f32[256,512]{0,1:T(8,128)S(1)}, u32[]{:S(2)}, u32[]{:S(2)}) collective-permute-start(f32[256,512]{0,1:T(8,128)S(1)} %get-tuple-element.1197), channel_id=1, source_target_pairs={{2,0},{3,1},{4,2},{5,3},{6,4},{7,5},{8,6},{9,7},{10,8},{11,9},{12,... | collective-permute-start | bytes 1572872 | tf_op jit(solution)/shard_map/ppermute | solution.py:16
  302.8 32.3 %collective-permute-start.9 = (f32[256,512]{0,1:T(8,128)S(1)}, f32[256,512]{0,1:T(8,128)S(1)}, u32[]{:S(2)}, u32[]{:S(2)}) collective-permute-start(f32[256,512]{0,1:T(8,128)S(1)} %get-tuple-element.1198), channel_id=1, source_target_pairs={{3,0},{4,1},{5,2},{6,3},{7,4},{8,5},{9,6},{10,7},{11,8},{12,9},{13... | collective-permute-start | bytes 1572872 | tf_op jit(solution)/shard_map/ppermute | solution.py:16
  312.1 23.0 %collective-permute-start.15 = (f32[256,512]{0,1:T(8,128)S(1)}, f32[256,512]{0,1:T(8,128)S(1)}, u32[]{:S(2)}, u32[]{:S(2)}) collective-permute-start(f32[256,512]{0,1:T(8,128)S(1)} %get-tuple-element.1199), channel_id=1, source_target_pairs={{0,4},{1,5},{2,6},{3,7},{4,8},{5,9},{6,10},{7,11},{8,12},{9,13},{1... | collective-permute-start | bytes 1572872 | tf_op jit(solution)/shard_map/ppermute | solution.py:16
  320.7 28.9 %collective-permute-start.14 = (f32[256,512]{0,1:T(8,128)S(1)}, f32[256,512]{0,1:T(8,128)S(1)}, u32[]{:S(2)}, u32[]{:S(2)}) collective-permute-start(f32[256,512]{0,1:T(8,128)S(1)} %get-tuple-element.1200), channel_id=1, source_target_pairs={{0,3},{1,4},{2,5},{3,6},{4,7},{5,8},{6,9},{7,10},{8,11},{9,12},{10... | collective-permute-start | bytes 1572872 | tf_op jit(solution)/shard_map/ppermute | solution.py:16
  351.0 124.5 %copy-start.6 = (bf16[256,192]{0,1:T(8,128)(2,1)S(1)}, bf16[256,192]{0,1:T(8,128)(2,1)}, u32[]{:S(2)}) copy-start(bf16[256,192]{0,1:T(8,128)(2,1)} %param.12) | copy-start | bytes 294916
  351.9 397.7 %all-reduce.6.cloned.1.call-start = ((), (), s32[]{:S(2)}) async-start(), calls=%async_computation.1 | async-start | bytes 1179648 | tf_op jit(solution)/shard_map/psum | solution.py:195
Sparse Core Ops, SparseCore 0:
  352.1 123.3 all-reduce.3
  478.6 270.9 all-reduce.5
where the time goes:
time: 761 us; the launch traced here: 758 us
  waiting for transfers between devices  364 us (48%)
  blocking collectives  141 us (19%)
  matrix products  100 us (13%)
  local copies, waits for them, and re-layouts  57.9 us (8%)
  starting transfers between devices  49.5 us (7%)
  other arithmetic  29 us (4%)
  between operations  15.1 us (2%)
    psum x1, waiting for transfers between devices, local(): grad_qkv = lax.psum(share, 'seq')  193 us
    psum x1, waiting for transfers between devices, local(): summed_rows = lax.psum(row_grads, 'cell')  123 us
    psum x1, blocking collectives, local(): grad_table = lax.psum(table_term, ('cell', 'seq'))  77.6 us
    psum x1, blocking collectives, local(): projected = lax.psum(partial_qkv, 'cell').astype(jnp.bfloat16)  63.3 us
    ppermute x16, starting transfers between devices, passed_along(): return lax.ppermute(block, axis, route)  49.5 us
    ppermute x16, waiting for transfers between devices, passed_along(): return lax.ppermute(block, axis, route)  47.2 us
    add x45, local copies, waits for them, and re-layouts, band_scores(): shaped = shaped + bias_terms[:, None]  26.1 us
    dot_general x18, matrix products, band_scores(): jnp.einsum('qhd,khd->qhk', query_rows, key_rows, preferred_element_type=j...  22.1 us
  transfers between devices with their start and end apart: 18, of which 10 were waited for; matrix products, arithmetic and copies ran while one was open for 1% of the time, Pallas kernels for 0%

commit v1 on v0

--- a/solution.py
+++ b/solution.py
@@ -185,7 +185,7 @@
             key_grads = key_grads + return_grads(segment, offset)
     query_grads = (q_total * factor).reshape(row_count, inner_width)
     row_grads = jnp.concatenate([query_grads, key_grads], axis=1)
-    summed_rows = lax.psum(row_grads, "cell")
+    summed_rows = jnp.sum(lax.all_gather(row_grads, "cell"), axis=0)
     share = jnp.dot(
         features.astype(jnp.float32).T,
         summed_rows,

time: 761 us -> 804 us (1.057)
  waiting for transfers between devices: 364 us -> 403 us
    all_gather x0 -> x1, waiting for transfers between devices: none -> 165 us  [local(): summed_rows = jnp.sum(lax.all_gather(row_grads, 'cell'), axis=0)]
    psum x1 -> x0, waiting for transfers between devices: 123 us -> none  [local(): summed_rows = lax.psum(row_grads, 'cell')]
    unnamed x32 -> x33, local copies, waits for them, and re-layouts: 10.7 us -> 16.5 us
where the time goes in v1:
time: 804 us; the launch traced here: 801 us
  waiting for transfers between devices  403 us (50%)
  blocking collectives  137 us (17%)
  matrix products  99 us (12%)
  local copies, waits for them, and re-layouts  63.8 us (8%)
  starting transfers between devices  49.7 us (6%)
  other arithmetic  31.2 us (4%)
  between operations  15.1 us (2%)
    psum x1, waiting for transfers between devices, local(): grad_qkv = lax.psum(share, 'seq')  191 us
    all_gather x1, waiting for transfers between devices, local(): summed_rows = jnp.sum(lax.all_gather(row_grads, 'cell'), axis=0)  165 us
    psum x1, blocking collectives, local(): grad_table = lax.psum(table_term, ('cell', 'seq'))  73.6 us
    psum x1, blocking collectives, local(): projected = lax.psum(partial_qkv, 'cell').astype(jnp.bfloat16)  63.3 us
    ppermute x16, starting transfers between devices, passed_along(): return lax.ppermute(block, axis, route)  49.4 us
    ppermute x16, waiting for transfers between devices, passed_along(): return lax.ppermute(block, axis, route)  47.3 us
    add x45, local copies, waits for them, and re-layouts, band_scores(): shaped = shaped + bias_terms[:, None]  26.1 us
    dot_general x18, matrix products, band_scores(): jnp.einsum('qhd,khd->qhk', query_rows, key_rows, preferred_element_type=j...  22.1 us
  transfers between devices with their start and end apart: 18, of which 10 were waited for; matrix products, arithmetic and copies ran while one was open for 1% of the time, Pallas kernels for 0%

profile of v1, /device:TPU:2, one launch (start us, length us, event | category | flops | bytes accessed | tf_op | source)
XLA Modules:
  0.0 800.9 jit_solution(9805088638674234868)
XLA Ops:
  7.3 1.6 copy-done
  10.0 63.3 %all-reduce.4 = bf16[256,768]{0,1:T(8,128)(2,1)} all-reduce(f32[256,768]{0,1:T(8,128)S(1)} %convolution_bitcast_fusion.6), channel_id=1, replica_groups=mesh['cell'=8,'seq'=32] {'cell'}, use_global_device_ids=true, to_apply=%region_0.0 | all-reduce | flops 196608 | bytes 1179648 | tf_op jit(solution)/shard_map/psum | solution.py:75
  74.4 5.8 collective-permute-start
  82.8 3.3 collective-permute-start.2
  86.0 4.0 collective-permute-start.1
  93.9 5.3 collective-permute-start.3
  100.2 2.1 collective-permute-done.1
  108.1 5.0 collective-permute-done.5
  114.1 1.6 fusion.66
  115.7 2.4 copy.86
  118.1 48.4 %while.54 = (s32[]{:T(128)}, f32[256,2]{0,1:T(2,128)S(1)}, f32[256,2]{0,1:T(2,128)S(1)}, s32[]{:T(128)}, bf16[2304,2,128]{2,0,1:T(8,128)(2,1)}, /*index=5*/bf16[...) while((s32[]{:T(128)}, f32[256,2]{0,1:T(2,128)S(1)}, ...), condition=%wide.region_6.7_spmd.clone, body=%wide.region_2.6_spmd.clone.sunk | while | flops 34921744 | bytes 3791994 | solution.py:112
  166.5 51.4 %while.55 = (s32[]{:T(128)}, f32[256,2,128]{0,2,1:T(8,128)}, bf16[2304,2,128]{0,2,1:T(8,128)(2,1)}, s32[]{:T(128)}, bf16[2304,2,128]{2,0,1:T(8,128)(2,1)}, /*ind...) while((s32[]{:T(128)}, f32[256,2,128]{0,2,1:T(8,128)}, ...), condition=%wide.region_9.10_spmd.clone, body=%wide.region_7.9_spmd.clone.sunk | while | flops 68473616 | bytes 3834520 | solution.py:124
  169.9 2.4 fusion.112
  175.5 2.4 fusion.112
  181.2 2.4 fusion.112
  186.9 2.4 fusion.112
  192.7 2.4 fusion.112
  198.4 2.4 fusion.112
  204.1 2.4 fusion.112
  209.8 2.4 fusion.112
  215.5 2.4 fusion.112
  219.0 2.4 broadcast_in_dim.354
  221.4 60.5 %while.56 = (s32[]{:T(128)}, f32[256,2,128]{0,2,1:T(8,128)S(1)}, f32[32,2]{0,1:T(2,128)S(1)}, f32[2304,512]{0,1:T(8,128)}, bf16[2304,2,128]{2,0,1:T(8,128)(2,1)}...) while((s32[]{:T(128)}, f32[256,2,128]{0,2,1:T(8,128)S(1)}, ...), condition=%wide.region_14.15_spmd.clone, body=%wide.region_11.14_spmd.clone.sunk | while | flops 505679744 | bytes 7515830 | solution.py:177
  225.4 1.4 fusion.125
  232.1 1.4 fusion.125
  238.9 1.4 fusion.125
  245.6 1.4 fusion.125
  252.3 1.4 fusion.125
  259.1 1.4 fusion.125
  265.8 1.4 fusion.125
  272.5 1.4 fusion.125
  279.2 1.4 fusion.125
  281.9 2.6 fusion.65
  285.9 4.4 collective-permute-start.13
  290.3 4.3 collective-permute-start.12
  297.2 5.6 collective-permute-done.8
  304.1 8.0 collective-permute-done.13
  312.1 8.6 %collective-permute-start.15 = (f32[256,512]{0,1:T(8,128)S(1)}, f32[256,512]{0,1:T(8,128)S(1)}, u32[]{:S(2)}, u32[]{:S(2)}) collective-permute-start(f32[256,512]{0,1:T(8,128)S(1)} %get-tuple-element.1199), channel_id=1, source_target_pairs={{0,4},{1,5},{2,6},{3,7},{4,8},{5,9},{6,10},{7,11},{8,12},{9,13},{1... | collective-permute-start | bytes 1572872 | tf_op jit(solution)/shard_map/ppermute | solution.py:16
  320.7 3.4 collective-permute-start.14
  324.1 10.8 %collective-permute-done.10 = f32[256,512]{0,1:T(8,128)S(1)} collective-permute-done((f32[256,512]{0,1:T(8,128)S(1)}, f32[256,512]{0,1:T(8,128)S(1)}, u32[]{:S(2)}, u32[]{:S(2)}) %collective-permute-start.10) | collective-permute-done | bytes 524320 | tf_op jit(solution)/shard_map/ppermute | solution.py:16
  335.2 14.4 %collective-permute-done.14 = f32[256,512]{0,1:T(8,128)S(1)} collective-permute-done((f32[256,512]{0,1:T(8,128)S(1)}, f32[256,512]{0,1:T(8,128)S(1)}, u32[]{:S(2)}, u32[]{:S(2)}) %collective-permute-start.14) | collective-permute-done | bytes 524320 | tf_op jit(solution)/shard_map/ppermute | solution.py:16
  352.1 164.8 %all-gather.3.cloned.1.call-done = f32[2048,768]{0,1:T(8,128)} async-done(((f32[256,768]{0,1:T(8,128)}), f32[2048,768]{0,1:T(8,128)}) %all-gather.3.cloned.1.call-update) | async-done | bytes 6291472 | tf_op jit(solution)/shard_map/all_gather | solution.py:188
  517.0 5.8 copy.98
  522.8 2.2 bitcast_reduce_fusion.1
  525.0 1.4 convolution_bitcast_fusion.7
  527.3 73.6 %psum.23 = f32[32,32,2]{1,2,0:T(2,128)} all-reduce(f32[32,32,2]{1,2,0:T(2,128)S(1)} %broadcast_select_fusion.1), channel_id=1, replica_groups=mesh['cell'=8,'seq'=32] {'cell','seq'}, use_global_device_ids=true, to_apply=%region_17.18 | all-reduce | flops 2048 | bytes 16384 | tf_op jit(solution)/shard_map/psum | solution.py:197
  600.9 191.3 %all-reduce.3.cloned.1.call-done = f32[192,768]{1,0:T(8,128)} async-done(((f32[192,768]{1,0:T(8,128)}), f32[192,768]{1,0:T(8,128)}) %all-reduce.3.cloned.1.call-update) | async-done | bytes 589840 | tf_op jit(solution)/shard_map/psum | solution.py:195
  792.1 1.9 copy.153
  (520 shorter events, 149.6 us)
Async XLA Ops:
  7.2 1.7 copy-start
  7.2 83.5 %copy-start.9 = (f32[32,32,2]{1,2,0:T(2,128)S(1)}, f32[32,32,2]{1,2,0:T(2,128)}, u32[]{:S(2)}) copy-start(f32[32,32,2]{1,2,0:T(2,128)} %param.16) | copy-start | bytes 24580
  7.2 86.6 %copy-start.8 = (bf16[1,256,256]{2,1,0:T(8,128)(2,1)S(1)}, bf16[1,256,256]{2,1,0:T(8,128)(2,1)}, u32[]{:S(2)}) copy-start(bf16[1,256,256]{2,1,0:T(8,128)(2,1)} %param.17) | copy-start | bytes 393220
  7.2 509.8 %all-gather.3.cloned.1.call-start = ((), (), s32[]{:S(2)}) async-start(), calls=%async_computation.1 | async-start | bytes 7077888 | tf_op jit(solution)/shard_map/all_gather | solution.py:188
  73.3 33.6 %copy-start.5 = (bf16[256,768]{0,1:T(8,128)(2,1)S(1)}, bf16[256,768]{0,1:T(8,128)(2,1)}, u32[]{:S(2)}) copy-start(bf16[256,768]{0,1:T(8,128)(2,1)} %all-reduce.4) | copy-start | bytes 1179652
  74.4 19.5 %collective-permute-start = (bf16[256,512]{0,1:T(8,128)(2,1)S(1)}, bf16[256,512]{0,1:T(8,128)(2,1)}, u32[]{:S(2)}, u32[]{:S(2)}) collective-permute-start(bf16[256,512]{0,1:T(8,128)(2,1)S(1)} %slice.52), channel_id=1, source_target_pairs={{0,4},{1,5},{2,6},{3,7},{4,8},{5,9},{6,10},{7,11},{8,12},{9,13},{1... | collective-permute-start | bytes 786440 | tf_op jit(solution)/shard_map/ppermute | solution.py:16
  80.2 33.9 %collective-permute-start.7 = (bf16[256,512]{0,1:T(8,128)(2,1)S(1)}, bf16[256,512]{0,1:T(8,128)(2,1)S(1)}, u32[]{:S(2)}, u32[]{:S(2)}) collective-permute-start(bf16[256,512]{0,1:T(8,128)(2,1)S(1)} %slice.52), channel_id=1, source_target_pairs={{4,0},{5,1},{6,2},{7,3},{8,4},{9,5},{10,6},{11,7},{12,8},{13,9},{1... | collective-permute-start | bytes 786440 | tf_op jit(solution)/shard_map/ppermute | solution.py:16
  81.5 31.7 %collective-permute-start.6 = (bf16[256,512]{0,1:T(8,128)(2,1)S(1)}, bf16[256,512]{0,1:T(8,128)(2,1)}, u32[]{:S(2)}, u32[]{:S(2)}) collective-permute-start(bf16[256,512]{0,1:T(8,128)(2,1)S(1)} %slice.52), channel_id=1, source_target_pairs={{3,0},{4,1},{5,2},{6,3},{7,4},{8,5},{9,6},{10,7},{11,8},{12,9},{13... | collective-permute-start | bytes 786440 | tf_op jit(solution)/shard_map/ppermute | solution.py:16
  82.8 21.8 %collective-permute-start.2 = (bf16[256,512]{0,1:T(8,128)(2,1)S(1)}, bf16[256,512]{0,1:T(8,128)(2,1)}, u32[]{:S(2)}, u32[]{:S(2)}) collective-permute-start(bf16[256,512]{0,1:T(8,128)(2,1)S(1)} %slice.52), channel_id=1, source_target_pairs={{0,2},{1,3},{2,4},{3,5},{4,6},{5,7},{6,8},{7,9},{8,10},{9,11},{10,... | collective-permute-start | bytes 786440 | tf_op jit(solution)/shard_map/ppermute | solution.py:16
  86.0 16.3 %collective-permute-start.1 = (bf16[256,512]{0,1:T(8,128)(2,1)S(1)}, bf16[256,512]{0,1:T(8,128)(2,1)}, u32[]{:S(2)}, u32[]{:S(2)}) collective-permute-start(bf16[256,512]{0,1:T(8,128)(2,1)S(1)} %slice.52), channel_id=1, source_target_pairs={{0,3},{1,4},{2,5},{3,6},{4,7},{5,8},{6,9},{7,10},{8,11},{9,12},{10... | collective-permute-start | bytes 786440 | tf_op jit(solution)/shard_map/ppermute | solution.py:16
  93.9 13.0 %collective-permute-start.3 = (bf16[256,512]{0,1:T(8,128)(2,1)S(1)}, bf16[256,512]{0,1:T(8,128)(2,1)S(1)}, u32[]{:S(2)}, u32[]{:S(2)}) collective-permute-start(bf16[256,512]{0,1:T(8,128)(2,1)S(1)} %slice.52), channel_id=1, source_target_pairs={{0,1},{1,2},{2,3},{3,4},{4,5},{5,6},{6,7},{7,8},{8,9},{9,10},{10,1... | collective-permute-start | bytes 786440 | tf_op jit(solution)/shard_map/ppermute | solution.py:16
  102.3 10.8 %collective-permute-start.5 = (bf16[256,512]{0,1:T(8,128)(2,1)S(1)}, bf16[256,512]{0,1:T(8,128)(2,1)S(1)}, u32[]{:S(2)}, u32[]{:S(2)}) collective-permute-start(bf16[256,512]{0,1:T(8,128)(2,1)S(1)} %slice.52), channel_id=1, source_target_pairs={{2,0},{3,1},{4,2},{5,3},{6,4},{7,5},{8,6},{9,7},{10,8},{11,9},{12,... | collective-permute-start | bytes 786440 | tf_op jit(solution)/shard_map/ppermute | solution.py:16
  104.6 3.4 collective-permute-start.4
  115.7 2.4 copy-start.7
  166.5 3.3 copy-start.1
  172.2 3.3 copy-start.1
  177.9 3.3 copy-start.1
  183.6 3.3 copy-start.1
  189.4 3.3 copy-start.1
  195.1 3.3 copy-start.1
  200.8 3.3 copy-start.1
  206.5 3.3 copy-start.1
  212.2 3.3 copy-start.1
  218.9 2.5 copy-start.2
  218.9 2.5 copy-start.3
  218.9 2.5 copy-start.4
  219.0 2.5 copy-start.10
  284.6 18.3 %collective-permute-start.8 = (f32[256,512]{0,1:T(8,128)S(1)}, f32[256,512]{0,1:T(8,128)S(1)}, u32[]{:S(2)}, u32[]{:S(2)}) collective-permute-start(f32[256,512]{0,1:T(8,128)S(1)} %get-tuple-element.1193), channel_id=1, source_target_pairs={{4,0},{5,1},{6,2},{7,3},{8,4},{9,5},{10,6},{11,7},{12,8},{13,9},{1... | collective-permute-start | bytes 1572872 | tf_op jit(solution)/shard_map/ppermute | solution.py:16
  285.9 26.2 %collective-permute-start.13 = (f32[256,512]{0,1:T(8,128)S(1)}, f32[256,512]{0,1:T(8,128)S(1)}, u32[]{:S(2)}, u32[]{:S(2)}) collective-permute-start(f32[256,512]{0,1:T(8,128)S(1)} %get-tuple-element.1194), channel_id=1, source_target_pairs={{0,2},{1,3},{2,4},{3,5},{4,6},{5,7},{6,8},{7,9},{8,10},{9,11},{10,... | collective-permute-start | bytes 1572872 | tf_op jit(solution)/shard_map/ppermute | solution.py:16
  290.3 30.4 %collective-permute-start.12 = (f32[256,512]{0,1:T(8,128)S(1)}, f32[256,512]{0,1:T(8,128)S(1)}, u32[]{:S(2)}, u32[]{:S(2)}) collective-permute-start(f32[256,512]{0,1:T(8,128)S(1)} %get-tuple-element.1195), channel_id=1, source_target_pairs={{0,1},{1,2},{2,3},{3,4},{4,5},{5,6},{6,7},{7,8},{8,9},{9,10},{10,1... | collective-permute-start | bytes 1572872 | tf_op jit(solution)/shard_map/ppermute | solution.py:16
  294.6 29.5 %collective-permute-start.11 = (f32[256,512]{0,1:T(8,128)S(1)}, f32[256,512]{0,1:T(8,128)S(1)}, u32[]{:S(2)}, u32[]{:S(2)}) collective-permute-start(f32[256,512]{0,1:T(8,128)S(1)} %get-tuple-element.1196), channel_id=1, source_target_pairs={{1,0},{2,1},{3,2},{4,3},{5,4},{6,5},{7,6},{8,7},{9,8},{10,9},{11,1... | collective-permute-start | bytes 1572872 | tf_op jit(solution)/shard_map/ppermute | solution.py:16
  295.9 39.0 %collective-permute-start.10 = (f32[256,512]{0,1:T(8,128)S(1)}, f32[256,512]{0,1:T(8,128)S(1)}, u32[]{:S(2)}, u32[]{:S(2)}) collective-permute-start(f32[256,512]{0,1:T(8,128)S(1)} %get-tuple-element.1197), channel_id=1, source_target_pairs={{2,0},{3,1},{4,2},{5,3},{6,4},{7,5},{8,6},{9,7},{10,8},{11,9},{12,... | collective-permute-start | bytes 1572872 | tf_op jit(solution)/shard_map/ppermute | solution.py:16
  302.8 32.3 %collective-permute-start.9 = (f32[256,512]{0,1:T(8,128)S(1)}, f32[256,512]{0,1:T(8,128)S(1)}, u32[]{:S(2)}, u32[]{:S(2)}) collective-permute-start(f32[256,512]{0,1:T(8,128)S(1)} %get-tuple-element.1198), channel_id=1, source_target_pairs={{3,0},{4,1},{5,2},{6,3},{7,4},{8,5},{9,6},{10,7},{11,8},{12,9},{13... | collective-permute-start | bytes 1572872 | tf_op jit(solution)/shard_map/ppermute | solution.py:16
  312.1 23.1 %collective-permute-start.15 = (f32[256,512]{0,1:T(8,128)S(1)}, f32[256,512]{0,1:T(8,128)S(1)}, u32[]{:S(2)}, u32[]{:S(2)}) collective-permute-start(f32[256,512]{0,1:T(8,128)S(1)} %get-tuple-element.1199), channel_id=1, source_target_pairs={{0,4},{1,5},{2,6},{3,7},{4,8},{5,9},{6,10},{7,11},{8,12},{9,13},{1... | collective-permute-start | bytes 1572872 | tf_op jit(solution)/shard_map/ppermute | solution.py:16
  320.7 28.9 %collective-permute-start.14 = (f32[256,512]{0,1:T(8,128)S(1)}, f32[256,512]{0,1:T(8,128)S(1)}, u32[]{:S(2)}, u32[]{:S(2)}) collective-permute-start(f32[256,512]{0,1:T(8,128)S(1)} %get-tuple-element.1200), channel_id=1, source_target_pairs={{0,3},{1,4},{2,5},{3,6},{4,7},{5,8},{6,9},{7,10},{8,11},{9,12},{10... | collective-permute-start | bytes 1572872 | tf_op jit(solution)/shard_map/ppermute | solution.py:16
  351.9 440.2 %all-reduce.3.cloned.1.call-start = ((), (), s32[]{:S(2)}) async-start(), calls=%async_computation | async-start | bytes 1179648 | tf_op jit(solution)/shard_map/psum | solution.py:195
  522.8 2.2 copy-start.6
Sparse Core Ops, SparseCore 0:
  352.0 164.8 all-gather.2
  526.5 265.5 all-reduce.2
